TPU v7x, 32 devices: a whole 2x2x4 slice. The times are simulated.
32 devices in a mesh: dp: 2 (over y), ctx: 2 (over x), exp: 8 (over z, core).
Axes of the slice: x: 2, y: 2, z: 4, core: 2. Of those that a mesh axis runs over, the one named last changes fastest.
Arguments:
- queries: bfloat16 [512, 4096], P(('dp', 'ctx'), 'exp'), parts along dimension 0, may hold values from -6 to 6
- key_vecs: bfloat16 [512, 4096], P(('dp', 'ctx'), 'exp'), parts along dimension 0, may hold values from -6 to 6
- values: bfloat16 [512, 4096], P(('dp', 'ctx'), 'exp'), parts along dimension 0, may hold values from -6 to 6
- residual: bfloat16 [512, 6144], P(('dp', 'ctx', 'exp')), parts along dimension 0, may hold values from -6 to 6
- out_weight: bfloat16 [4096, 6144], P('exp', 'ctx'), may hold values from -0.09375 to 0.09375
- router_weight: bfloat16 [6144, 4], replicated, may hold values from -0.078125 to 0.078125
- expert_ids: int32 [512, 2], P(('dp', 'ctx', 'exp')), parts along dimension 0, may hold values from 0 to 3, all different within a row; in each aligned block of 16 rows (0 to 15, 16 to 31, ...) at most 12 rows name the same one
- gate_weight: bfloat16 [8, 6144, 2304], P('exp', None, 'ctx'), may hold values from -0.078125 to 0.078125
- up_weight: bfloat16 [8, 6144, 2304], P('exp', None, 'ctx'), may hold values from -0.078125 to 0.078125
- down_weight: bfloat16 [8, 2304, 6144], P('exp', 'ctx'), may hold values from -0.09375 to 0.09375
Outputs:
- layer_out: bfloat16 [512, 6144], P(('dp', 'ctx', 'exp')), parts along dimension 0
There are 2 independent parts, one for each index of `dp`. A program takes and returns all parts, laid end to end along the dimension named above; an argument that names none is the same for every part. Nothing has to cross between parts.
Inputs may be any that keep to these rules, and one draw needn't show every extreme that they name: `expert_ids`: the two experts of a row differ. In each aligned block of 16 rows (the rows of one device) no expert is named by more than 12 rows.
All inputs are finite; a program needn't handle non-finite values.
Results may differ from a plain program's by a relative error of at most 0.017.
Values may be sent and summed in bfloat16 or wider, within the bound.
A program may use at most 128 MiB of HBM per device.

v0:
```python
import jax
import jax.numpy as jnp
from jax import lax
from jax.sharding import PartitionSpec as P

HEAD = 128


EPSILON = 1e-06


def carried_in(value, axis, combine, identity):
    peers, position = (lax.axis_size(axis), lax.axis_index(axis))
    everything = lax.all_gather(value.astype(jnp.bfloat16), axis)
    start = jnp.broadcast_to(jnp.asarray(identity, value.dtype), value.shape)

    def lap(k, before):
        reached = k < position
        new = combine(before, everything[k].astype(value.dtype))
        return jnp.where(reached, new, before)

    return lax.fori_loop(0, peers, lap, start)


def expert_rows(tokens, gate_half, up_half, down_half):
    gate_part = jnp.dot(tokens, gate_half, preferred_element_type=jnp.float32)
    up_part = jnp.dot(tokens, up_half, preferred_element_type=jnp.float32)
    hidden = (jax.nn.silu(gate_part) * up_part).astype(jnp.bfloat16)
    return jnp.dot(hidden, down_half, preferred_element_type=jnp.float32)


def add_states(first, second):
    return first + second


def per_device(
    queries,
    key_vecs,
    values,
    residual,
    out_weight,
    router_weight,
    expert_ids,
    gate_weight,
    up_weight,
    down_weight,
):
    ctx_count = lax.axis_size("ctx")
    exp_count = lax.axis_size("exp")
    span_len, local_width = queries.shape
    head_local = local_width // HEAD
    q_heads = queries.reshape(span_len, head_local, HEAD)
    k_heads = key_vecs.reshape(span_len, head_local, HEAD)
    v_heads = values.reshape(span_len, head_local, HEAD)
    scores = jnp.einsum("thd,shd->hts", q_heads, k_heads, preferred_element_type=jnp.float32)
    causal = jnp.arange(span_len)[:, None] >= jnp.arange(span_len)[None, :]
    masked = jnp.where(causal[None], scores, jnp.float32(0.0)).astype(jnp.bfloat16)
    within = jnp.einsum("hts,shd->thd", masked, v_heads, preferred_element_type=jnp.float32)
    own_state = jnp.einsum("shd,she->hde", k_heads, v_heads, preferred_element_type=jnp.float32)
    earlier = carried_in(own_state, "ctx", add_states, jnp.zeros_like(own_state))
    carried = jnp.einsum(
        "thd,hde->the", q_heads, earlier.astype(jnp.bfloat16), preferred_element_type=jnp.float32
    )
    attended = within + carried
    normed = attended * lax.rsqrt(jnp.mean(attended * attended, axis=-1, keepdims=True) + EPSILON)
    heads_out = normed.astype(jnp.bfloat16).reshape(span_len, local_width)
    projected = jnp.dot(
        heads_out,
        lax.all_gather(out_weight, "ctx", axis=1, tiled=True),
        preferred_element_type=jnp.float32,
    )
    mixed = lax.psum_scatter(
        projected.astype(jnp.bfloat16), "exp", scatter_dimension=0, tiled=True
    ).astype(jnp.float32)
    hidden_in = (residual.astype(jnp.float32) + mixed).astype(jnp.bfloat16)
    token_count, model_width = hidden_in.shape
    expert_count = router_weight.shape[1]
    capacity = min(token_count, 3 * token_count // expert_count)
    logits = jnp.dot(hidden_in, router_weight, preferred_element_type=jnp.float32)
    chosen = (expert_ids[:, :, None] == jnp.arange(expert_count)[None, None, :]).astype(jnp.float32)
    picked = jnp.sum(chosen * logits[:, None, :], axis=-1)
    leading = jax.nn.sigmoid(picked[:, 0] - picked[:, 1])
    mixing = jnp.stack([leading, 1.0 - leading], axis=1)
    entries = chosen.reshape(2 * token_count, expert_count)
    position = jnp.arange(2 * token_count)
    earlier_mask = (position[:, None] > position[None, :]).astype(jnp.float32)
    ranks = jnp.dot(earlier_mask, entries, precision=lax.Precision.HIGHEST)
    slot_of = jnp.sum(ranks * entries, axis=-1).reshape(token_count, 2)
    slot_hot = (
        slot_of[:, :, None] == jnp.arange(capacity).astype(jnp.float32)[None, None, :]
    ).astype(jnp.float32)
    placed = chosen[:, :, :, None] * slot_hot[:, :, None, :]
    dispatch = jnp.sum(placed, axis=1).astype(jnp.bfloat16)
    combine = jnp.sum(placed * mixing[:, :, None, None], axis=1)
    packed = jnp.einsum(
        "tes,td->esd", dispatch, hidden_in, preferred_element_type=jnp.float32
    ).astype(jnp.bfloat16)
    outgoing = jnp.repeat(packed, 2, axis=0)
    gate_half = gate_weight[0]
    up_half = up_weight[0]
    down_half = down_weight[0]
    fanned = jnp.broadcast_to(outgoing[None], (ctx_count,) + outgoing.shape).reshape(
        ctx_count * exp_count, capacity, model_width
    )
    arrived = lax.all_to_all(fanned, ("ctx", "exp"), split_axis=0, concat_axis=0, tiled=True)
    flattened = arrived.reshape(-1, model_width)
    partial_value = expert_rows(flattened, gate_half, up_half, down_half).reshape(arrived.shape)
    reduced = lax.psum_scatter(
        partial_value.reshape(ctx_count * exp_count * capacity, model_width).astype(jnp.bfloat16),
        "ctx",
        scatter_dimension=0,
        tiled=True,
    ).astype(jnp.float32)
    returned = lax.all_to_all(
        reduced.reshape(exp_count, capacity, model_width).astype(jnp.bfloat16),
        "exp",
        split_axis=0,
        concat_axis=0,
        tiled=True,
    ).astype(jnp.float32)
    summed = jnp.sum(returned.reshape(expert_count, 2, capacity, model_width), axis=1)
    expert_out = jnp.einsum(
        "tes,esd->td",
        combine,
        summed,
        precision=lax.Precision.HIGHEST,
        preferred_element_type=jnp.float32,
    )
    return (hidden_in.astype(jnp.float32) + expert_out).astype(jnp.bfloat16)


def solution(mesh):
    in_specs = (
        P(("dp", "ctx"), "exp"),
        P(("dp", "ctx"), "exp"),
        P(("dp", "ctx"), "exp"),
        P(("dp", "ctx", "exp"), None),
        P("exp", "ctx"),
        P(),
        P(("dp", "ctx", "exp"), None),
        P("exp", None, "ctx"),
        P("exp", None, "ctx"),
        P("exp", "ctx", None),
    )
    out_specs = P(("dp", "ctx", "exp"), None)
    return jax.shard_map(
        per_device, mesh=mesh, in_specs=in_specs, out_specs=out_specs, check_vma=False
    )
```

profile of v0, /device:TPU:0, one launch (start us, length us, event | category | flops | bytes accessed | tf_op | source)
XLA Modules:
  0.0 318.2 jit_solution(11882675133803179610)
XLA Ops:
  6.5 0.7 all-gather.3.cloned.1.call-update
  7.3 0.2 copy-done.6
  7.5 0.1 copy.50
  7.6 0.2 convolution_convert_fusion.2
  7.8 7.1 %all-gather = bf16[8,128,128]{2,1,0:T(8,128)(2,1)S(1)} all-gather(bf16[4,128,128]{2,1,0:T(8,128)(2,1)S(1)} %convolution_convert_fusion.2), channel_id=2, replica_groups=mesh['dp'=2,'ctx'=2,'exp'=8] {'ctx'}, dimensions={0}, use_global_device_ids=true | all-gather | bytes 393216 | tf_op jit(solution)/shard_map/all_gather | solution.py:14
  14.9 0.3 convolution_bitcast_fusion.2
  15.3 0.3 while.14
  15.3 0.1 add_select_fusion.2
  15.4 0.1 add_select_fusion.2
  15.6 0.3 multiply_reduce_fusion
  15.9 76.2 %all-gather.3.cloned.1.call-done = bf16[512,6144]{1,0:T(8,128)(2,1)} async-done(((bf16[512,3072]{1,0:T(8,128)(2,1)}), bf16[512,6144]{1,0:T(8,128)(2,1)}) %all-gather.3.cloned.1.call-update) | async-done | bytes 6291472 | tf_op jit(solution)/shard_map/all_gather | solution.py:69
  92.0 5.0 %convolution_convert_fusion = bf16[128,6144]{1,0:T(8,128)(2,1)} fusion(bf16[128,512]{0,1:T(8,128)(2,1)S(1)} %bitcast.85, bf16[512,6144]{1,0:T(8,128)(2,1)} %all-gather.3.cloned.1.call-done), kind=kOutput, calls=%fused_computation.8 | convolution fusion | flops 806092800 | bytes 7995392 | tf_op jit(solution)/shard_map/dot_general | solution.py:67
  97.1 0.1 copy.45
  97.2 0.1 eq.49
  97.3 0.1 fusion.19
  97.4 0.1 eq.53
  97.5 0.1 copy.46
  97.7 33.7 %reduce-scatter.3.cloned.1.call-done = bf16[16,6144]{1,0:T(8,128)(2,1)} async-done(((bf16[128,6144]{1,0:T(8,128)(2,1)}), bf16[16,6144]{1,0:T(8,128)(2,1)}) %reduce-scatter.3.cloned.1.call-update) | async-done | bytes 196624 | tf_op jit(solution)/shard_map/reduce_scatter | solution.py:72
  131.4 1.1 fusion.40
  132.6 1.3 convolution_convert_fusion.1
  133.9 0.2 broadcast_in_dim.20
  134.1 0.4 broadcast_in_dim.22
  134.4 72.9 %all_to_all.10 = bf16[16,12,6144]{2,1,0:T(8,128)(2,1)S(1)} all-to-all(bf16[16,12,6144]{2,1,0:T(8,128)(2,1)S(1)} %bitcast.80), channel_id=1, replica_groups=mesh['dp'=2,'ctx'=2,'exp'=8] {'ctx','exp'}, dimensions={0} | all-to-all | bytes 4718592 | tf_op jit(solution)/shard_map/all_to_all | solution.py:105
  207.3 2.1 reshape.71
  209.5 9.1 %fusion.4 = f32[192,1152]{1,0:T(8,128)S(1)} fusion(bf16[192,6144]{1,0:T(8,128)(2,1)} %reshape.71, bf16[1,6144,1152]{2,1,0:T(8,128)(2,1)} %param.19), kind=kOutput, calls=%fused_computation.5 | convolution fusion | flops 2717908992 | bytes 17399808 | tf_op jit(solution)/shard_map/dot_general | solution.py:26
  218.6 8.5 %fusion.14 = bf16[192,1152]{1,0:T(8,128)(2,1)S(1)} fusion(bf16[192,6144]{1,0:T(8,128)(2,1)S(1)} %copy-done.2, bf16[1,6144,1152]{2,1,0:T(8,128)(2,1)} %param.20, f32[192,1152]{1,0:T(8,128)S(1)} %fusion.4), kind=kOutput, calls=%fused_computation.15 | convolution fusion | flops 2719236096 | bytes 17842176 | tf_op jit(solution)/shard_map/dot_general | solution.py:27
  227.1 4.6 %fusion.6 = bf16[192,6144]{1,0:T(8,128)(2,1)} fusion(bf16[192,1152]{1,0:T(8,128)(2,1)S(1)} %fusion.14, bf16[1,1152,6144]{2,1,0:T(8,128)(2,1)S(1)} %bitcast.87), kind=kOutput, calls=%fused_computation.7 | convolution fusion | flops 2719088640 | bytes 16957440 | tf_op jit(solution)/shard_map/dot_general | solution.py:29
  231.7 34.2 %reduce-scatter.5.cloned.1.call-done = bf16[96,6144]{1,0:T(8,128)(2,1)} async-done(((bf16[192,6144]{1,0:T(8,128)(2,1)}), bf16[96,6144]{1,0:T(8,128)(2,1)}) %reduce-scatter.5.cloned.1.call-update) | async-done | bytes 1179664 | tf_op jit(solution)/shard_map/reduce_scatter | solution.py:108
  266.0 1.4 convert_element_type.97
  267.4 42.4 %all_to_all.11 = bf16[8,12,6144]{2,1,0:T(8,128)(2,1)S(1)} all-to-all(bf16[8,12,6144]{2,1,0:T(8,128)(2,1)S(1)} %convert_element_type.97), channel_id=1, replica_groups=mesh['dp'=2,'ctx'=2,'exp'=8] {'exp'}, dimensions={0} | all-to-all | bytes 2359296 | tf_op jit(solution)/shard_map/all_to_all | solution.py:114
  309.8 0.3 convert_reduce_fusion
  310.1 1.6 fusion.10
  (42 shorter events, 0.4 us)
Async XLA Ops:
  6.5 8.4 %copy-start = (bf16[128,512]{1,0:T(8,128)(2,1)S(1)}, bf16[128,512]{1,0:T(8,128)(2,1)}, u32[]{:S(2)}) copy-start(bf16[128,512]{1,0:T(8,128)(2,1)} %param.12) | copy-start | bytes 393220
  6.5 0.9 copy-start.6
  6.5 1.1 copy-start.5
  6.5 85.5 %all-gather.3.cloned.1.call-start = ((), (), s32[]{:S(2)}) async-start(), calls=%async_computation.4 | async-start | bytes 9437184 | tf_op jit(solution)/shard_map/all_gather | solution.py:69
  7.3 124.1 %reduce-scatter.3.cloned.1.call-start = ((), (), s32[]{:S(2)}) async-start(), calls=%async_computation.5 | async-start | bytes 1769472 | tf_op jit(solution)/shard_map/reduce_scatter | solution.py:72
  92.0 5.1 %copy-start.7 = (s32[16,2]{0,1:T(2,128)S(1)}, s32[16,2]{0,1:T(2,128)}, u32[]{:S(2)}) copy-start(s32[16,2]{0,1:T(2,128)} %param.18) | copy-start | bytes 388
  92.0 39.4 %copy-start.3 = (bf16[16,6144]{1,0:T(8,128)(2,1)S(1)}, bf16[16,6144]{1,0:T(8,128)(2,1)}, u32[]{:S(2)}) copy-start(bf16[16,6144]{1,0:T(8,128)(2,1)} %param.15) | copy-start | bytes 589828
  92.0 39.4 %copy-start.8 = (bf16[6144,4]{0,1:T(4,128)(2,1)S(1)}, bf16[6144,4]{0,1:T(4,128)(2,1)}, u32[]{:S(2)}) copy-start(bf16[6144,4]{0,1:T(4,128)(2,1)} %param.17) | copy-start | bytes 147460
  97.0 168.9 %reduce-scatter.5.cloned.1.call-start = ((), (), s32[]{:S(2)}) async-start(), calls=%async_computation.6 | async-start | bytes 3538944 | tf_op jit(solution)/shard_map/reduce_scatter | solution.py:108
  209.5 9.1 %copy-start.2 = (bf16[192,6144]{1,0:T(8,128)(2,1)S(1)}, bf16[192,6144]{1,0:T(8,128)(2,1)}, u32[]{:S(2)}) copy-start(bf16[192,6144]{1,0:T(8,128)(2,1)} %reshape.71) | copy-start | bytes 7077892
  209.5 17.6 %slice-start = ((s8[14155776]{0:T(1024)(128)(4,1)}), s8[4194304]{0:T(1024)(128)(4,1)S(1)}, s32[]{:S(2)}) async-start(s8[14155776]{0:T(1024)(128)(4,1)} %bitcast.86), calls=%async_computation.7 | async-start | bytes 8388608
  209.5 17.6 %slice-start.1 = ((s8[14155776]{0:T(1024)(128)(4,1)}), s8[4194304]{0:T(1024)(128)(4,1)S(1)}, s32[]{:S(2)}) async-start(s8[14155776]{0:T(1024)(128)(4,1)} %bitcast.86), calls=%async_computation.8 | async-start | bytes 8388608
  218.6 8.5 %slice-start.2 = ((s8[14155776]{0:T(1024)(128)(4,1)}), s8[4194304]{0:T(1024)(128)(4,1)S(1)}, s32[]{:S(2)}) async-start(s8[14155776]{0:T(1024)(128)(4,1)} %bitcast.86), calls=%async_computation.9 | async-start | bytes 8388608
  218.6 8.5 %slice-start.3 = ((s8[14155776]{0:T(1024)(128)(4,1)}), s8[1572864]{0:T(1024)(128)(4,1)S(1)}, s32[]{:S(2)}) async-start(s8[14155776]{0:T(1024)(128)(4,1)} %bitcast.86), calls=%async_computation.10 | async-start | bytes 3145728
  267.4 42.7 %copy-start.4 = (bf16[16,6144]{1,0:T(8,128)(2,1)S(1)}, bf16[16,6144]{1,0:T(8,128)(2,1)}, u32[]{:S(2)}) copy-start(bf16[16,6144]{1,0:T(8,128)(2,1)} %reduce-scatter.3.cloned.1.call-done) | copy-start | bytes 589828
  267.4 44.3 %copy-start.1 = (bf16[128,512]{1,0:T(8,128)(2,1)S(1)}, bf16[128,512]{1,0:T(8,128)(2,1)}, u32[]{:S(2)}) copy-start(bf16[128,512]{1,0:T(8,128)(2,1)} %param.12) | copy-start | bytes 393220
Sparse Core Ops, SparseCore 0:
  8.9 83.0 all-gather.2
  97.2 34.2 reduce-scatter.2
  231.9 34.0 reduce-scatter.4
where the time goes:
time: 318 us
  waiting for transfers between devices  145 us (46%)
  blocking collectives  122 us (38%)
  matrix products  32 us (10%)
  between operations  13.4 us (4%)
  local copies, waits for them, and re-layouts  4.71 us (1%)
    all_gather x1, waiting for transfers between devices, per_device(): lax.all_gather(out_weight, 'ctx', axis=1, tiled=True)  76.2 us
    all_to_all x1, blocking collectives, per_device(): lax.all_to_all(fanned, ('ctx', 'exp'), split_axis=0, concat_axis=0, tiled...  72.9 us
    all_to_all x1, blocking collectives, per_device(): lax.all_to_all(reduced.reshape(exp_count, capacity, model_width).astype(j...  42.4 us
    reduce_scatter x1, waiting for transfers between devices, per_device(): lax.psum_scatter(partial_value.reshape(ctx_count * exp_count * capacity,...  34.2 us
    reduce_scatter x1, waiting for transfers between devices, per_device(): lax.psum_scatter(projected.astype(jnp.bfloat16), 'exp', scatter_dimension...  33.7 us
    dot_general x1, matrix products, expert_rows(): gate_part = jnp.dot(tokens, gate_half, preferred_element_type=jnp.float32)  9.1 us
    dot_general x1, matrix products, expert_rows(): up_part = jnp.dot(tokens, up_half, preferred_element_type=jnp.float32)  8.46 us
    all_gather x1, blocking collectives, carried_in(): everything = lax.all_gather(value.astype(jnp.bfloat16), axis)  7.09 us
  transfers between devices with their start and end apart: 3, of which 3 were waited for; matrix products, arithmetic and copies ran while one was open for 1% of the time, Pallas kernels for 0%

commit v1 on v0

--- a/solution.py
+++ b/solution.py
@@ -1,6 +1,8 @@
 import jax
 import jax.numpy as jnp
 from jax import lax
+from jax.experimental import pallas as pl
+from jax.experimental.pallas import tpu as pltpu
 from jax.sharding import PartitionSpec as P
 
 HEAD = 128
@@ -129,7 +131,366 @@
     return (hidden_in.astype(jnp.float32) + expert_out).astype(jnp.bfloat16)
 
 
+BF, F32 = jnp.bfloat16, jnp.float32
+ROWS = 16
+
+
+def layer_kernel(
+    q_ref, k_ref, v_ref, res_ref, wo_hbm, router_ref, ids_ref, gate_hbm, up_hbm, down_hbm,
+    out_ref,
+    wy, gate, up, down, state, state_in, within, heads, res_in, term, pair_in, pair, ring_in,
+    every, gate_sum, up_sum, hidden, core_in, side_out, side_in, ready, back,
+    w_sem, att_s, att_r, pair_s, pair_r, ring_s, ring_r,
+    gz_s, gz_r, gx_s, gx_r, gc_s, gc_r, yc_s, yc_r, yx_s, yx_r, yz_s, yz_r,
+):
+    h, e = lax.axis_index("ctx"), lax.axis_index("exp")
+    z, c = e // 2, lax.rem(e, 2)
+    half = res_ref.shape[1] // 2
+    width = q_ref.shape[1]
+    span = q_ref.shape[0]
+    hid = gate.shape[1]
+    chips = 4
+    order = (2, 1, 3, 0)
+    side = {"ctx": 1 - h, "exp": e}
+    core = {"ctx": h, "exp": 2 * z + 1 - c}
+
+    def at_z(dz):
+        return lax.rem(z + dz, chips)
+
+    def from_z(dz):
+        return lax.rem(z + chips - dz, chips)
+
+    def to(dz, other):
+        return {"ctx": h, "exp": 2 * at_z(dz) + (1 - c if other else c)}
+
+    started = []
+
+    def link(src, dst, s, r, dev):
+        return pltpu.make_async_remote_copy(
+            src_ref=src, dst_ref=dst, send_sem=s, recv_sem=r, device_id=dev,
+            device_id_type=pl.DeviceIdType.MESH,
+        )
+
+    def send(*args):
+        copy = link(*args)
+        copy.start()
+        started.append(copy)
+        return copy
+
+    load_wo = pltpu.make_async_copy(wo_hbm, wy, w_sem.at[0])
+    load_wo.start()
+    loads = [
+        pltpu.make_async_copy(gate_hbm.at[0], gate, w_sem.at[1]),
+        pltpu.make_async_copy(up_hbm.at[0], up, w_sem.at[2]),
+        pltpu.make_async_copy(down_hbm.at[0], down, w_sem.at[3]),
+    ]
+
+    barrier = pltpu.get_barrier_semaphore()
+    pl.semaphore_signal(barrier, inc=1, device_id=side, device_id_type=pl.DeviceIdType.MESH)
+    for dz in range(chips):
+        for other in (False, True):
+            if dz or other:
+                pl.semaphore_signal(
+                    barrier, inc=1, device_id=to(dz, other), device_id_type=pl.DeviceIdType.MESH
+                )
+    pl.semaphore_wait(barrier, 2 * chips)
+
+    count = width // HEAD
+    for i in range(count):
+        cols = slice(i * HEAD, (i + 1) * HEAD)
+        own = lax.dot_general(
+            k_ref[:, cols], v_ref[:, cols], (((0,), (0,)), ((), ())), preferred_element_type=F32
+        )
+        state[cols, :] = own.astype(BF)
+    state_copy = send(state, state_in, att_s.at[0], att_r.at[0], side)
+    peer_cols = pl.ds(pl.multiple_of((1 - h) * half, half), half)
+    my_cols = pl.ds(pl.multiple_of(h * half, half), half)
+    res_copy = send(res_ref.at[:, peer_cols], res_in, att_s.at[1], att_r.at[1], side)
+    keep = lax.broadcasted_iota(jnp.int32, (span, span), 0) >= lax.broadcasted_iota(
+        jnp.int32, (span, span), 1
+    )
+    for i in range(count):
+        cols = slice(i * HEAD, (i + 1) * HEAD)
+        scores = lax.dot_general(
+            q_ref[:, cols], k_ref[:, cols], (((1,), (1,)), ((), ())), preferred_element_type=F32
+        )
+        masked = jnp.where(keep, scores, 0.0).astype(BF)
+        within[:, cols] = jnp.dot(masked, v_ref[:, cols], preferred_element_type=F32)
+    state_copy.wait_recv()
+    has_past = (h > 0).astype(F32)
+    for i in range(count):
+        cols = slice(i * HEAD, (i + 1) * HEAD)
+        carried = jnp.dot(q_ref[:, cols], state_in[cols, :], preferred_element_type=F32)
+        attended = within[:, cols] + carried * has_past
+        normed = attended * lax.rsqrt(
+            jnp.mean(attended * attended, axis=-1, keepdims=True) + EPSILON
+        )
+        heads[h, :, cols] = normed.astype(BF)
+    heads_copy = send(heads.at[h], heads.at[h], att_s.at[2], att_r.at[2], side)
+    for load in loads:
+        load.start()
+    load_wo.wait()
+
+    tile = 256
+
+    def project(b):
+        @pl.loop(0, half // tile)
+        def _(n):
+            cols = pl.ds(pl.multiple_of(n * tile, tile), tile)
+            part = jnp.dot(heads[b], wy[:, cols], preferred_element_type=F32).astype(BF)
+            term[b, :, :, cols] = part.reshape(span // ROWS, ROWS, tile)
+
+    project(h)
+    link(heads.at[1 - h], heads.at[1 - h], att_s.at[2], att_r.at[2], side).wait_recv()
+    project(1 - h)
+
+    for dz in order:
+        send(
+            term.at[:, 2 * at_z(dz) + 1 - c], pair_in.at[dz], pair_s.at[dz], pair_r.at[dz], core
+        )
+    for dz in order:
+        link(
+            term.at[:, 2 * at_z(dz) + 1 - c], pair_in.at[dz], pair_s.at[dz], pair_r.at[dz], core
+        ).wait_recv()
+        if dz:
+            both = term[:, 2 * at_z(dz) + c].astype(F32) + pair_in[dz].astype(F32)
+            pair[dz - 1] = both.astype(BF)
+            send(
+                pair.at[dz - 1], ring_in.at[dz - 1], ring_s.at[dz - 1], ring_r.at[dz - 1],
+                to(dz, False),
+            )
+    res_copy.wait_recv()
+    for dz in (1, 2, 3):
+        link(
+            pair.at[dz - 1], ring_in.at[dz - 1], ring_s.at[dz - 1], ring_r.at[dz - 1],
+            to(dz, False),
+        ).wait_recv()
+
+    def mixed(b):
+        total = term[b, e].astype(F32) + pair_in[0, b].astype(F32)
+        for dz in (1, 2, 3):
+            total = total + ring_in[dz - 1, b].astype(F32)
+        return total
+
+    every[h, h, e] = (res_ref[:, my_cols].astype(F32) + mixed(h)).astype(BF)
+    every[h, 1 - h, e] = (res_in[...].astype(F32) + mixed(1 - h)).astype(BF)
+
+    def piece(side_half, owner):
+        return every.at[side_half, :, owner]
+
+    mine = piece(h, e)
+    for dz in (2, 1, 3):
+        send(mine, mine, gz_s.at[dz - 1], gz_r.at[dz - 1], to(dz, False))
+    send(mine, mine, gx_s.at[0], gx_r.at[0], side)
+    send(mine, mine, gc_s.at[0], gc_r.at[0], core)
+
+    for dz in (1, 3, 2):
+        owner = 2 * from_z(dz) + c
+        got = piece(h, owner)
+        link(got, got, gz_s.at[dz - 1], gz_r.at[dz - 1], to(dz, False)).wait_recv()
+        send(got, got, gx_s.at[dz], gx_r.at[dz], side)
+        send(got, got, gc_s.at[dz], gc_r.at[dz], core)
+
+    def pass_on(dz):
+        got = piece(1 - h, 2 * from_z(dz) + c)
+        link(got, got, gx_s.at[dz], gx_r.at[dz], side).wait_recv()
+        send(got, got, gc_s.at[4 + dz], gc_r.at[4 + dz], core)
+
+    def from_core(side_half, slot, dz):
+        got = piece(side_half, 2 * from_z(dz) + 1 - c)
+        link(got, got, gc_s.at[slot], gc_r.at[slot], core).wait_recv()
+
+    def tiles(body):
+        whole = hid // tile
+
+        @pl.loop(0, whole)
+        def _(n):
+            body(pl.ds(pl.multiple_of(n * tile, tile), tile))
+
+        if hid % tile:
+            body(pl.ds(whole * tile, hid % tile))
+
+    def product(side_half, weight, cols):
+        rows = pl.ds(pl.multiple_of(side_half * half, half), half)
+        return jnp.dot(
+            every[side_half].reshape(2 * span, half), weight[rows, cols],
+            preferred_element_type=F32,
+        )
+
+    for dz in range(chips):
+        from_core(h, dz, dz)
+    pass_on(0)
+    pass_on(1)
+    loads[0].wait()
+
+    def first_gate(cols):
+        gate_sum[:, cols] = product(h, gate, cols)
+
+    def first_up(cols):
+        up_sum[:, cols] = product(h, up, cols)
+
+    tiles(first_gate)
+    pass_on(3)
+    loads[1].wait()
+    tiles(first_up)
+    pass_on(2)
+    for dz in range(chips):
+        from_core(1 - h, 4 + dz, dz)
+
+    def second(cols):
+        g = gate_sum[:, cols] + product(1 - h, gate, cols)
+        u = up_sum[:, cols] + product(1 - h, up, cols)
+        hidden[:, cols] = (g / (1.0 + jnp.exp(-g)) * u).astype(BF)
+
+    tiles(second)
+    loads[2].wait()
+
+    def lower(side_half):
+        @pl.loop(0, half // tile)
+        def _(n):
+            cols = pl.ds(pl.multiple_of(side_half * half + n * tile, tile), tile)
+            part = jnp.dot(hidden[...], down[:, cols], preferred_element_type=F32)
+            rows = pl.ds(pl.multiple_of(side_half * 2 * span, 2 * span), 2 * span)
+            wy[rows, pl.ds(pl.multiple_of(n * tile, tile), tile)] = part.astype(BF)
+
+    def rows_of(side_half, b, dz):
+        first = side_half * 2 * span + b * span + 2 * ROWS * at_z(dz)
+        return pl.ds(pl.multiple_of(first, 2 * ROWS), 2 * ROWS)
+
+    def core_link(dz, b):
+        return (
+            wy.at[rows_of(1 - c, b, dz)], core_in.at[dz, b], yc_s.at[dz, b], yc_r.at[dz, b], core
+        )
+
+    def away(dz):
+        return core_link(dz, 1 - h)
+
+    lower(1 - c)
+    for dz in order:
+        for b in range(2):
+            send(*core_link(dz, b))
+    lower(c)
+    for dz in order:
+        for b in range(2):
+            link(*core_link(dz, b)).wait_recv()
+        side_out[dz] = (
+            wy[rows_of(c, 1 - h, dz)].astype(F32) + core_in[dz, 1 - h].astype(F32)
+        ).astype(BF)
+        send(side_out.at[dz], side_in.at[dz], yx_s.at[dz], yx_r.at[dz], side)
+
+    def out_link(dz, other):
+        if dz:
+            part = 1 - c if other else c
+            src = ready.at[dz, pl.ds(pl.multiple_of(part * ROWS, ROWS), ROWS)]
+        else:
+            src = ready.at[dz, pl.ds(pl.multiple_of((1 - c) * ROWS, ROWS), ROWS)]
+        o = int(other)
+        return (src, back.at[dz, o], yz_s.at[dz, o], yz_r.at[dz, o], to(dz, other))
+
+    for dz in order:
+        link(side_out.at[dz], side_in.at[dz], yx_s.at[dz], yx_r.at[dz], side).wait_recv()
+        ready[dz] = (
+            wy[rows_of(c, h, dz)].astype(F32)
+            + core_in[dz, h].astype(F32)
+            + side_in[dz].astype(F32)
+        ).astype(BF)
+        for other in (False, True):
+            if dz or other:
+                send(*out_link(dz, other))
+
+    logits = jnp.zeros((ROWS, router_ref.shape[0]), F32)
+    for s in range(2):
+        logits = logits + lax.dot_general(
+            every[s, h, e], router_ref[:, s * half:(s + 1) * half],
+            (((1,), (1,)), ((), ())), preferred_element_type=F32,
+        )
+    lanes = lax.broadcasted_iota(jnp.int32, logits.shape, 1)
+    one = (ids_ref[:, 0:1] == lanes).astype(F32)
+    two = (ids_ref[:, 1:2] == lanes).astype(F32)
+    gap = jnp.sum((one - two) * logits, axis=1, keepdims=True)
+    leading = 1.0 / (1.0 + jnp.exp(-gap))
+    share = leading * one + (1.0 - leading) * two
+
+    def weight_of(dz):
+        return jnp.sum(jnp.where(lanes == from_z(dz), share, 0.0), axis=1, keepdims=True)
+
+    weights = [weight_of(dz) for dz in range(chips)]
+    for other in (False, True):
+        for dz in order:
+            if dz or other:
+                link(*out_link(dz, other)).wait_recv()
+        part = 1 - c if other else c
+        total = every[part, h, e].astype(F32)
+        for dz in range(chips):
+            if dz or other:
+                value = back[dz, int(other)]
+            else:
+                value = ready[0, pl.ds(pl.multiple_of(c * ROWS, ROWS), ROWS)]
+            total = total + weights[dz] * value.astype(F32)
+        out_ref[:, pl.ds(pl.multiple_of(part * half, half), half)] = total.astype(BF)
+    for copy in started:
+        copy.wait_send()
+
+
+def per_device_fused(
+    queries, key_vecs, values, residual, out_weight, router_weight, expert_ids,
+    gate_weight, up_weight, down_weight,
+):
+    span, width = queries.shape
+    half = out_weight.shape[1]
+    model = residual.shape[1]
+    hid = gate_weight.shape[2]
+    blocks = span // ROWS
+    vmem, sem = pltpu.VMEM, pltpu.SemaphoreType.DMA
+    in_vmem = pl.BlockSpec(memory_space=pltpu.VMEM)
+    in_hbm = pl.BlockSpec(memory_space=pl.ANY)
+    return pl.pallas_call(
+        layer_kernel,
+        out_shape=jax.ShapeDtypeStruct(residual.shape, BF),
+        in_specs=[in_vmem] * 4 + [in_hbm] + [in_vmem] * 2 + [in_hbm] * 3,
+        out_specs=in_vmem,
+        scratch_shapes=[
+            vmem((width, half), BF),
+            vmem((model, hid), BF),
+            vmem((model, hid), BF),
+            vmem((hid, model), BF),
+            vmem((width, HEAD), BF),
+            vmem((width, HEAD), BF),
+            vmem((span, width), F32),
+            vmem((2, span, width), BF),
+            vmem((ROWS, half), BF),
+            vmem((2, blocks, ROWS, half), BF),
+            vmem((4, 2, ROWS, half), BF),
+            vmem((3, 2, ROWS, half), BF),
+            vmem((3, 2, ROWS, half), BF),
+            vmem((2, 2, blocks, ROWS, half), BF),
+            vmem((2 * span, hid), F32),
+            vmem((2 * span, hid), F32),
+            vmem((2 * span, hid), BF),
+            vmem((4, 2, 2 * ROWS, half), BF),
+            vmem((4, 2 * ROWS, half), BF),
+            vmem((4, 2 * ROWS, half), BF),
+            vmem((4, 2 * ROWS, half), BF),
+            vmem((4, 2, ROWS, half), BF),
+            sem((4,)), sem((3,)), sem((3,)), sem((4,)), sem((4,)), sem((3,)), sem((3,)),
+            sem((3,)), sem((3,)), sem((4,)), sem((4,)), sem((8,)), sem((8,)),
+            sem((4, 2)), sem((4, 2)), sem((4,)), sem((4,)), sem((4, 2)), sem((4, 2)),
+        ],
+        compiler_params=pltpu.CompilerParams(
+            collective_id=0, has_side_effects=True, vmem_limit_bytes=VMEM_BYTES
+        ),
+    )(
+        queries, key_vecs, values, residual, out_weight, router_weight.T, expert_ids,
+        gate_weight, up_weight, down_weight,
+    )
+
+
+VMEM_BYTES = 66 * 1000 * 1000
+
+
 def solution(mesh):
+    fused = mesh.shape["ctx"] == 2 and mesh.shape["exp"] == 8
+    body = per_device_fused if fused else per_device
     in_specs = (
         P(("dp", "ctx"), "exp"),
         P(("dp", "ctx"), "exp"),
@@ -144,5 +505,5 @@
     )
     out_specs = P(("dp", "ctx", "exp"), None)
     return jax.shard_map(
-        per_device, mesh=mesh, in_specs=in_specs, out_specs=out_specs, check_vma=False
-    )
+        body, mesh=mesh, in_specs=in_specs, out_specs=out_specs, check_vma=False
+    )

time: 318 us -> 113 us (0.36)
  waiting for transfers between devices: 145 us -> 0 us
  blocking collectives: 122 us -> 0 us
  Pallas kernels: 0 us -> 110 us
  matrix products: 32 us -> 0 us
  between operations: 13.4 us -> 0.01 us
    all_to_all x2 -> x0, blocking collectives: 115 us -> none  [the longest x1 72.9 us: per_device(): lax.all_to_all(fanned, ('ctx', 'exp'), split_axis=0, concat_axis=0, tiled...]
    pallas_call x0 -> x1, Pallas kernels: none -> 110 us  [per_device_fused(): pl.pallas_call(layer_kernel, out_shape=jax.ShapeDtypeStruct(residual.shap...]
    all_gather x1 -> x0, waiting for transfers between devices: 76.2 us -> none  [per_device(): lax.all_gather(out_weight, 'ctx', axis=1, tiled=True)]
    reduce_scatter x2 -> x0, waiting for transfers between devices: 68 us -> none  [the longest x1 34.2 us: per_device(): lax.psum_scatter(partial_value.reshape(ctx_count * exp_count * capacity,...]
    dot_general x11 -> x0, matrix products: 32 us -> none  [the longest x1 9.1 us: expert_rows(): gate_part = jnp.dot(tokens, gate_half, preferred_element_type=jnp.float32)]
    all_gather x1 -> x0, blocking collectives: 7.09 us -> none  [carried_in(): everything = lax.all_gather(value.astype(jnp.bfloat16), axis)]
  transfers between devices with their start and end apart: 3 -> 0, of which waited for: 3 -> 0; matrix products, arithmetic and copies ran while one was open for 1% -> 0% of each run, Pallas kernels for 0% -> 0%
where the time goes in v1:
time: 113 us
  Pallas kernels  110 us (97%)
  local copies, waits for them, and re-layouts  2.97 us (3%)
    pallas_call x1, Pallas kernels, per_device_fused(): pl.pallas_call(layer_kernel, out_shape=jax.ShapeDtypeStruct(residual.shap...  110 us
    unnamed x2, local copies, waits for them, and re-layouts  2.97 us

profile of v1, /device:TPU:0, one launch (start us, length us, event | category | flops | bytes accessed | tf_op | source)
XLA Modules:
  0.0 112.5 jit_solution(4782043712991904799)
XLA Ops:
  0.0 1.4 %copy.11.ids_ref = s32[16,2]{1,0:T(8,128)} copy(s32[16,2]{0,1:T(2,128)} %param.16) | data formatting | bytes 256 | tf_op args[6]
  1.4 109.6 %shard_map.100 = bf16[16,6144]{1,0:T(8,128)(2,1)} custom-call(bf16[128,512]{1,0:T(8,128)(2,1)} %q_ref.1, bf16[128,512]{1,0:T(8,128)(2,1)} %k_ref.1, bf16[128,512]{1,0:T(8,128)(2,1)} %v_ref.1, bf16[16,6144]{1,0:T(8,128)(2,1)} %res_ref.1, bf16[512,3072]{1,0:T(8,128)(2,1)} %wo_hbm.1, bf16[4,6144]{1,0:T(4,128)(2,1)} %bitcast.1, s32[16,2]{1,0:T(8,128)} %copy.11.ids_ref, ...), custom_call_target="tpu_custom_call" | custom-call | tf_op jit(solution)/shard_map/pallas_call | solution.py:447
  110.9 1.6 %copy.13 = bf16[16,6144]{1,0:T(8,128)(2,1)} copy(bf16[16,6144]{1,0:T(8,128)(2,1)} %shard_map.100) | data formatting | bytes 393216

commit v2 on v1

--- a/solution.py
+++ b/solution.py
@@ -140,7 +140,7 @@
     out_ref,
     wy, gate, up, down, state, state_in, within, heads, res_in, term, pair_in, pair, ring_in,
     every, gate_sum, up_sum, hidden, core_in, side_out, side_in, ready, back,
-    w_sem, att_s, att_r, pair_s, pair_r, ring_s, ring_r,
+    w_sem, state_s, state_r, heads_s, heads_r, att_s, att_r, pair_s, pair_r, ring_s, ring_r,
     gz_s, gz_r, gx_s, gx_r, gc_s, gc_r, yc_s, yc_r, yx_s, yx_r, yz_s, yz_r,
 ):
     h, e = lax.axis_index("ctx"), lax.axis_index("exp")
@@ -196,16 +196,26 @@
     pl.semaphore_wait(barrier, 2 * chips)
 
     count = width // HEAD
-    for i in range(count):
-        cols = slice(i * HEAD, (i + 1) * HEAD)
-        own = lax.dot_general(
-            k_ref[:, cols], v_ref[:, cols], (((0,), (0,)), ((), ())), preferred_element_type=F32
-        )
-        state[cols, :] = own.astype(BF)
-    state_copy = send(state, state_in, att_s.at[0], att_r.at[0], side)
-    peer_cols = pl.ds(pl.multiple_of((1 - h) * half, half), half)
-    my_cols = pl.ds(pl.multiple_of(h * half, half), half)
-    res_copy = send(res_ref.at[:, peer_cols], res_in, att_s.at[1], att_r.at[1], side)
+    def state_link(i):
+        rows = pl.ds(i * HEAD, HEAD)
+        return link(state.at[rows], state_in.at[rows], state_s.at[i], state_r.at[i], side)
+
+    def heads_link(i, b):
+        cols = pl.ds(i * HEAD, HEAD)
+        part = heads.at[b, :, cols]
+        return link(part, part, heads_s.at[i], heads_r.at[i], side)
+
+    @pl.when(h == 0)
+    def _():
+        for i in range(count):
+            cols = slice(i * HEAD, (i + 1) * HEAD)
+            own = lax.dot_general(
+                k_ref[:, cols], v_ref[:, cols], (((0,), (0,)), ((), ())),
+                preferred_element_type=F32,
+            )
+            state[cols, :] = own.astype(BF)
+            state_link(i).start()
+
     keep = lax.broadcasted_iota(jnp.int32, (span, span), 0) >= lax.broadcasted_iota(
         jnp.int32, (span, span), 1
     )
@@ -216,17 +226,25 @@
         )
         masked = jnp.where(keep, scores, 0.0).astype(BF)
         within[:, cols] = jnp.dot(masked, v_ref[:, cols], preferred_element_type=F32)
-    state_copy.wait_recv()
-    has_past = (h > 0).astype(F32)
     for i in range(count):
         cols = slice(i * HEAD, (i + 1) * HEAD)
-        carried = jnp.dot(q_ref[:, cols], state_in[cols, :], preferred_element_type=F32)
-        attended = within[:, cols] + carried * has_past
+
+        @pl.when(h == 1)
+        def _():
+            state_link(i).wait_recv()
+            within[:, cols] += jnp.dot(
+                q_ref[:, cols], state_in[cols, :], preferred_element_type=F32
+            )
+
+        attended = within[:, cols]
         normed = attended * lax.rsqrt(
             jnp.mean(attended * attended, axis=-1, keepdims=True) + EPSILON
         )
         heads[h, :, cols] = normed.astype(BF)
-    heads_copy = send(heads.at[h], heads.at[h], att_s.at[2], att_r.at[2], side)
+        heads_link(i, h).start()
+    peer_cols = pl.ds(pl.multiple_of((1 - h) * half, half), half)
+    my_cols = pl.ds(pl.multiple_of(h * half, half), half)
+    res_copy = send(res_ref.at[:, peer_cols], res_in, att_s.at[0], att_r.at[0], side)
     for load in loads:
         load.start()
     load_wo.wait()
@@ -240,35 +258,37 @@
             part = jnp.dot(heads[b], wy[:, cols], preferred_element_type=F32).astype(BF)
             term[b, :, :, cols] = part.reshape(span // ROWS, ROWS, tile)
 
+    def core_term(dz, b):
+        src = term.at[b, 2 * at_z(dz) + 1 - c]
+        return (src, pair_in.at[dz, b], pair_s.at[dz, b], pair_r.at[dz, b], core)
+
+    def ring_term(dz, b):
+        k = dz - 1
+        return (
+            pair.at[k, b], ring_in.at[k, b], ring_s.at[k, b], ring_r.at[k, b], to(dz, False)
+        )
+
+    def scatter(b):
+        for dz in order:
+            send(*core_term(dz, b))
+        for dz in order:
+            link(*core_term(dz, b)).wait_recv()
+            if dz:
+                both = term[b, 2 * at_z(dz) + c].astype(F32) + pair_in[dz, b].astype(F32)
+                pair[dz - 1, b] = both.astype(BF)
+                send(*ring_term(dz, b))
+
     project(h)
-    link(heads.at[1 - h], heads.at[1 - h], att_s.at[2], att_r.at[2], side).wait_recv()
+    scatter(h)
+    for i in range(count):
+        heads_link(i, 1 - h).wait_recv()
     project(1 - h)
-
-    for dz in order:
-        send(
-            term.at[:, 2 * at_z(dz) + 1 - c], pair_in.at[dz], pair_s.at[dz], pair_r.at[dz], core
-        )
-    for dz in order:
-        link(
-            term.at[:, 2 * at_z(dz) + 1 - c], pair_in.at[dz], pair_s.at[dz], pair_r.at[dz], core
-        ).wait_recv()
-        if dz:
-            both = term[:, 2 * at_z(dz) + c].astype(F32) + pair_in[dz].astype(F32)
-            pair[dz - 1] = both.astype(BF)
-            send(
-                pair.at[dz - 1], ring_in.at[dz - 1], ring_s.at[dz - 1], ring_r.at[dz - 1],
-                to(dz, False),
-            )
+    scatter(1 - h)
     res_copy.wait_recv()
-    for dz in (1, 2, 3):
-        link(
-            pair.at[dz - 1], ring_in.at[dz - 1], ring_s.at[dz - 1], ring_r.at[dz - 1],
-            to(dz, False),
-        ).wait_recv()
-
     def mixed(b):
         total = term[b, e].astype(F32) + pair_in[0, b].astype(F32)
         for dz in (1, 2, 3):
+            link(*ring_term(dz, b)).wait_recv()
             total = total + ring_in[dz - 1, b].astype(F32)
         return total
 
@@ -278,27 +298,64 @@
     def piece(side_half, owner):
         return every.at[side_half, :, owner]
 
-    mine = piece(h, e)
-    for dz in (2, 1, 3):
-        send(mine, mine, gz_s.at[dz - 1], gz_r.at[dz - 1], to(dz, False))
-    send(mine, mine, gx_s.at[0], gx_r.at[0], side)
-    send(mine, mine, gc_s.at[0], gc_r.at[0], core)
-
-    for dz in (1, 3, 2):
-        owner = 2 * from_z(dz) + c
-        got = piece(h, owner)
-        link(got, got, gz_s.at[dz - 1], gz_r.at[dz - 1], to(dz, False)).wait_recv()
-        send(got, got, gx_s.at[dz], gx_r.at[dz], side)
-        send(got, got, gc_s.at[dz], gc_r.at[dz], core)
-
-    def pass_on(dz):
-        got = piece(1 - h, 2 * from_z(dz) + c)
-        link(got, got, gx_s.at[dz], gx_r.at[dz], side).wait_recv()
-        send(got, got, gc_s.at[4 + dz], gc_r.at[4 + dz], core)
-
-    def from_core(side_half, slot, dz):
-        got = piece(side_half, 2 * from_z(dz) + 1 - c)
-        link(got, got, gc_s.at[slot], gc_r.at[slot], core).wait_recv()
+    steps = []
+    for k in range(1, chips):
+        steps.append((z >= k, z - k, k - 1, 1))
+        steps.append((z + k < chips, z + k, chips + k - 2, -1))
+
+    def along(side_way, owner, slot):
+        got = piece(h, 2 * owner + c)
+        dev = {"ctx": h, "exp": 2 * (z + side_way) + c}
+        return link(got, got, gz_s.at[slot], gz_r.at[slot], dev)
+
+    def goes_on(side_way):
+        return (z + side_way >= 0) & (z + side_way < chips)
+
+    def to_side(owner):
+        got = piece(h, 2 * owner + c)
+        return link(got, got, gx_s.at[owner], gx_r.at[owner], side)
+
+    def from_side(owner):
+        got = piece(1 - h, 2 * owner + c)
+        return link(got, got, gx_s.at[owner], gx_r.at[owner], side)
+
+    def to_core(side_half, first, owner):
+        got = piece(side_half, 2 * owner + c)
+        return link(got, got, gc_s.at[first + owner], gc_r.at[first + owner], core)
+
+    for side_way, slot in ((1, 0), (-1, chips - 1)):
+        @pl.when(goes_on(side_way))
+        def _():
+            along(side_way, z, slot).start()
+
+    to_side(z).start()
+    to_core(h, 0, z).start()
+
+    for there, owner, slot, side_way in steps:
+        @pl.when(there)
+        def _():
+            along(side_way, owner, slot).wait_recv()
+
+            if slot % (chips - 1) < chips - 2:
+                @pl.when(goes_on(side_way))
+                def _():
+                    along(side_way, owner, slot + 1).start()
+
+            to_side(owner).start()
+            to_core(h, 0, owner).start()
+
+    def pass_on(owner):
+        from_side(owner).wait_recv()
+        to_core(1 - h, chips, owner).start()
+
+    def pass_step(there, owner):
+        @pl.when(there)
+        def _():
+            pass_on(owner)
+
+    def from_core(side_half, first, owner):
+        got = piece(side_half, 2 * owner + 1 - c)
+        link(got, got, gc_s.at[first + owner], gc_r.at[first + owner], core).wait_recv()
 
     def tiles(body):
         whole = hid // tile
@@ -317,10 +374,11 @@
             preferred_element_type=F32,
         )
 
-    for dz in range(chips):
-        from_core(h, dz, dz)
-    pass_on(0)
-    pass_on(1)
+    pass_on(z)
+    for there, owner, _, _ in steps[:2]:
+        pass_step(there, owner)
+    for owner in range(chips):
+        from_core(h, 0, owner)
     loads[0].wait()
 
     def first_gate(cols):
@@ -330,12 +388,14 @@
         up_sum[:, cols] = product(h, up, cols)
 
     tiles(first_gate)
-    pass_on(3)
+    for there, owner, _, _ in steps[2:4]:
+        pass_step(there, owner)
     loads[1].wait()
     tiles(first_up)
-    pass_on(2)
-    for dz in range(chips):
-        from_core(1 - h, 4 + dz, dz)
+    for there, owner, _, _ in steps[4:]:
+        pass_step(there, owner)
+    for owner in range(chips):
+        from_core(1 - h, chips, owner)
 
     def second(cols):
         g = gate_sum[:, cols] + product(1 - h, gate, cols)
@@ -362,17 +422,13 @@
             wy.at[rows_of(1 - c, b, dz)], core_in.at[dz, b], yc_s.at[dz, b], yc_r.at[dz, b], core
         )
 
-    def away(dz):
-        return core_link(dz, 1 - h)
-
     lower(1 - c)
-    for dz in order:
-        for b in range(2):
+    for b in (1 - h, h):
+        for dz in order:
             send(*core_link(dz, b))
     lower(c)
     for dz in order:
-        for b in range(2):
-            link(*core_link(dz, b)).wait_recv()
+        link(*core_link(dz, 1 - h)).wait_recv()
         side_out[dz] = (
             wy[rows_of(c, 1 - h, dz)].astype(F32) + core_in[dz, 1 - h].astype(F32)
         ).astype(BF)
@@ -389,6 +445,7 @@
 
     for dz in order:
         link(side_out.at[dz], side_in.at[dz], yx_s.at[dz], yx_r.at[dz], side).wait_recv()
+        link(*core_link(dz, h)).wait_recv()
         ready[dz] = (
             wy[rows_of(c, h, dz)].astype(F32)
             + core_in[dz, h].astype(F32)
@@ -398,21 +455,25 @@
             if dz or other:
                 send(*out_link(dz, other))
 
-    logits = jnp.zeros((ROWS, router_ref.shape[0]), F32)
+    logits = jnp.zeros((router_ref.shape[0], ROWS), F32)
     for s in range(2):
         logits = logits + lax.dot_general(
-            every[s, h, e], router_ref[:, s * half:(s + 1) * half],
+            router_ref[:, s * half:(s + 1) * half], every[s, h, e],
             (((1,), (1,)), ((), ())), preferred_element_type=F32,
         )
-    lanes = lax.broadcasted_iota(jnp.int32, logits.shape, 1)
-    one = (ids_ref[:, 0:1] == lanes).astype(F32)
-    two = (ids_ref[:, 1:2] == lanes).astype(F32)
-    gap = jnp.sum((one - two) * logits, axis=1, keepdims=True)
+    lines = lax.broadcasted_iota(jnp.int32, logits.shape, 0)
+    one = (ids_ref[0:1, :] == lines).astype(F32)
+    two = (ids_ref[1:2, :] == lines).astype(F32)
+    gap = jnp.sum((one - two) * logits, axis=0, keepdims=True)
     leading = 1.0 / (1.0 + jnp.exp(-gap))
     share = leading * one + (1.0 - leading) * two
+    diagonal = lax.broadcasted_iota(jnp.int32, (ROWS, ROWS), 0) == lax.broadcasted_iota(
+        jnp.int32, (ROWS, ROWS), 1
+    )
 
     def weight_of(dz):
-        return jnp.sum(jnp.where(lanes == from_z(dz), share, 0.0), axis=1, keepdims=True)
+        row = jnp.sum(jnp.where(lines == from_z(dz), share, 0.0), axis=0, keepdims=True)
+        return jnp.sum(jnp.where(diagonal, row, 0.0), axis=1, keepdims=True)
 
     weights = [weight_of(dz) for dz in range(chips)]
     for other in (False, True):
@@ -431,6 +492,29 @@
     for copy in started:
         copy.wait_send()
 
+    @pl.when(h == 0)
+    def _():
+        for i in range(count):
+            state_link(i).wait_send()
+
+    for i in range(count):
+        heads_link(i, h).wait_send()
+    for side_way, slot in ((1, 0), (-1, chips - 1)):
+        @pl.when(goes_on(side_way))
+        def _():
+            along(side_way, z, slot).wait_send()
+
+    for there, owner, slot, side_way in steps:
+        if slot % (chips - 1) < chips - 2:
+            @pl.when(there & goes_on(side_way))
+            def _():
+                along(side_way, owner, slot + 1).wait_send()
+
+    for owner in range(chips):
+        to_side(owner).wait_send()
+        to_core(h, 0, owner).wait_send()
+        to_core(1 - h, chips, owner).wait_send()
+
 
 def per_device_fused(
     queries, key_vecs, values, residual, out_weight, router_weight, expert_ids,
@@ -441,6 +525,7 @@
     model = residual.shape[1]
     hid = gate_weight.shape[2]
     blocks = span // ROWS
+    count = width // HEAD
     vmem, sem = pltpu.VMEM, pltpu.SemaphoreType.DMA
     in_vmem = pl.BlockSpec(memory_space=pltpu.VMEM)
     in_hbm = pl.BlockSpec(memory_space=pl.ANY)
@@ -472,15 +557,16 @@
             vmem((4, 2 * ROWS, half), BF),
             vmem((4, 2 * ROWS, half), BF),
             vmem((4, 2, ROWS, half), BF),
-            sem((4,)), sem((3,)), sem((3,)), sem((4,)), sem((4,)), sem((3,)), sem((3,)),
-            sem((3,)), sem((3,)), sem((4,)), sem((4,)), sem((8,)), sem((8,)),
+            sem((4,)), sem((count,)), sem((count,)), sem((count,)), sem((count,)), sem((1,)), sem((1,)),
+            sem((4, 2)), sem((4, 2)), sem((3, 2)), sem((3, 2)),
+            sem((6,)), sem((6,)), sem((4,)), sem((4,)), sem((8,)), sem((8,)),
             sem((4, 2)), sem((4, 2)), sem((4,)), sem((4,)), sem((4, 2)), sem((4, 2)),
         ],
         compiler_params=pltpu.CompilerParams(
             collective_id=0, has_side_effects=True, vmem_limit_bytes=VMEM_BYTES
         ),
     )(
-        queries, key_vecs, values, residual, out_weight, router_weight.T, expert_ids,
+        queries, key_vecs, values, residual, out_weight, router_weight.T, expert_ids.T,
         gate_weight, up_weight, down_weight,
     )
 

time: 113 us -> 96.1 us (0.85)
  Pallas kernels: 110 us -> 93.4 us
  local copies, waits for them, and re-layouts: 2.97 us -> 1.62 us
    pallas_call x1, Pallas kernels: 110 us -> 93.4 us  [per_device_fused(): pl.pallas_call(layer_kernel, out_shape=jax.ShapeDtypeStruct(residual.shap...]
    unnamed x2 -> x1, local copies, waits for them, and re-layouts: 2.97 us -> 1.62 us
where the time goes in v2:
time: 96.1 us; the launch traced here: 95.1 us
  Pallas kernels  93.4 us (97%)
  local copies, waits for them, and re-layouts  1.62 us (2%)
    pallas_call x1, Pallas kernels, per_device_fused(): pl.pallas_call(layer_kernel, out_shape=jax.ShapeDtypeStruct(residual.shap...  93.4 us

profile of v2, /device:TPU:0, one launch (start us, length us, event | category | flops | bytes accessed | tf_op | source)
XLA Modules:
  0.0 95.1 jit_solution(18014617055738967776)
XLA Ops:
  0.0 93.4 %shard_map.100 = bf16[16,6144]{1,0:T(8,128)(2,1)} custom-call(bf16[128,512]{1,0:T(8,128)(2,1)} %q_ref.1, bf16[128,512]{1,0:T(8,128)(2,1)} %k_ref.1, bf16[128,512]{1,0:T(8,128)(2,1)} %v_ref.1, bf16[16,6144]{1,0:T(8,128)(2,1)} %res_ref.1, bf16[512,3072]{1,0:T(8,128)(2,1)} %wo_hbm.1, bf16[4,6144]{1,0:T(4,128)(2,1)} %bitcast.2, s32[2,16]{1,0:T(2,128)} %bitcast.3, ...), custom_call_target="tpu_custom_call" | custom-call | tf_op jit(solution)/shard_map/pallas_call | solution.py:532
  93.4 1.6 %copy.12 = bf16[16,6144]{1,0:T(8,128)(2,1)} copy(bf16[16,6144]{1,0:T(8,128)(2,1)} %shard_map.100) | data formatting | bytes 393216

commit v3 on v2

--- a/solution.py
+++ b/solution.py
@@ -284,7 +284,6 @@
         heads_link(i, 1 - h).wait_recv()
     project(1 - h)
     scatter(1 - h)
-    res_copy.wait_recv()
     def mixed(b):
         total = term[b, e].astype(F32) + pair_in[0, b].astype(F32)
         for dz in (1, 2, 3):
@@ -292,70 +291,76 @@
             total = total + ring_in[dz - 1, b].astype(F32)
         return total
 
-    every[h, h, e] = (res_ref[:, my_cols].astype(F32) + mixed(h)).astype(BF)
-    every[h, 1 - h, e] = (res_in[...].astype(F32) + mixed(1 - h)).astype(BF)
-
-    def piece(side_half, owner):
-        return every.at[side_half, :, owner]
-
     steps = []
     for k in range(1, chips):
         steps.append((z >= k, z - k, k - 1, 1))
         steps.append((z + k < chips, z + k, chips + k - 2, -1))
 
-    def along(side_way, owner, slot):
-        got = piece(h, 2 * owner + c)
+    def along(side_way, owner, slot, b):
+        got = every.at[h, b, 2 * owner + c]
         dev = {"ctx": h, "exp": 2 * (z + side_way) + c}
-        return link(got, got, gz_s.at[slot], gz_r.at[slot], dev)
+        return link(got, got, gz_s.at[slot, b], gz_r.at[slot, b], dev)
 
     def goes_on(side_way):
         return (z + side_way >= 0) & (z + side_way < chips)
 
-    def to_side(owner):
-        got = piece(h, 2 * owner + c)
-        return link(got, got, gx_s.at[owner], gx_r.at[owner], side)
-
-    def from_side(owner):
-        got = piece(1 - h, 2 * owner + c)
-        return link(got, got, gx_s.at[owner], gx_r.at[owner], side)
-
-    def to_core(side_half, first, owner):
-        got = piece(side_half, 2 * owner + c)
-        return link(got, got, gc_s.at[first + owner], gc_r.at[first + owner], core)
-
-    for side_way, slot in ((1, 0), (-1, chips - 1)):
-        @pl.when(goes_on(side_way))
-        def _():
-            along(side_way, z, slot).start()
-
-    to_side(z).start()
-    to_core(h, 0, z).start()
-
-    for there, owner, slot, side_way in steps:
-        @pl.when(there)
-        def _():
-            along(side_way, owner, slot).wait_recv()
-
-            if slot % (chips - 1) < chips - 2:
-                @pl.when(goes_on(side_way))
-                def _():
-                    along(side_way, owner, slot + 1).start()
-
-            to_side(owner).start()
-            to_core(h, 0, owner).start()
-
-    def pass_on(owner):
-        from_side(owner).wait_recv()
-        to_core(1 - h, chips, owner).start()
-
-    def pass_step(there, owner):
-        @pl.when(there)
-        def _():
-            pass_on(owner)
-
-    def from_core(side_half, first, owner):
-        got = piece(side_half, 2 * owner + 1 - c)
-        link(got, got, gc_s.at[first + owner], gc_r.at[first + owner], core).wait_recv()
+    def to_side(owner, b):
+        got = every.at[h, b, 2 * owner + c]
+        return link(got, got, gx_s.at[owner, b], gx_r.at[owner, b], side)
+
+    def from_side(owner, b):
+        got = every.at[1 - h, b, 2 * owner + c]
+        return link(got, got, gx_s.at[owner, b], gx_r.at[owner, b], side)
+
+    def to_core(side_half, first, owner, b):
+        got = every.at[side_half, b, 2 * owner + c]
+        return link(got, got, gc_s.at[first + owner, b], gc_r.at[first + owner, b], core)
+
+    def spread(b):
+        for side_way, slot in ((1, 0), (-1, chips - 1)):
+            @pl.when(goes_on(side_way))
+            def _():
+                along(side_way, z, slot, b).start()
+
+        to_side(z, b).start()
+        to_core(h, 0, z, b).start()
+
+    def forward(some, b):
+        for there, owner, slot, side_way in some:
+            @pl.when(there)
+            def _():
+                along(side_way, owner, slot, b).wait_recv()
+
+                if slot % (chips - 1) < chips - 2:
+                    @pl.when(goes_on(side_way))
+                    def _():
+                        along(side_way, owner, slot + 1, b).start()
+
+                to_side(owner, b).start()
+                to_core(h, 0, owner, b).start()
+
+    def pass_on(owner, b):
+        from_side(owner, b).wait_recv()
+        to_core(1 - h, chips, owner, b).start()
+
+    def pass_steps(some, b):
+        for there, owner, _, _ in some:
+            @pl.when(there)
+            def _():
+                pass_on(owner, b)
+
+    def from_core(side_half, first, owner, b):
+        got = every.at[side_half, b, 2 * owner + 1 - c]
+        link(got, got, gc_s.at[first + owner, b], gc_r.at[first + owner, b], core).wait_recv()
+
+    every[h, h, e] = (res_ref[:, my_cols].astype(F32) + mixed(h)).astype(BF)
+    spread(h)
+    forward(steps[:2], h)
+    res_copy.wait_recv()
+    every[h, 1 - h, e] = (res_in[...].astype(F32) + mixed(1 - h)).astype(BF)
+    spread(1 - h)
+    forward(steps[2:], h)
+    forward(steps, 1 - h)
 
     def tiles(body):
         whole = hid // tile
@@ -374,11 +379,12 @@
             preferred_element_type=F32,
         )
 
-    pass_on(z)
-    for there, owner, _, _ in steps[:2]:
-        pass_step(there, owner)
-    for owner in range(chips):
-        from_core(h, 0, owner)
+    pass_on(z, 1 - h)
+    pass_steps(steps, 1 - h)
+    pass_on(z, h)
+    for b in range(2):
+        for owner in range(chips):
+            from_core(h, 0, owner, b)
     loads[0].wait()
 
     def first_gate(cols):
@@ -388,14 +394,13 @@
         up_sum[:, cols] = product(h, up, cols)
 
     tiles(first_gate)
-    for there, owner, _, _ in steps[2:4]:
-        pass_step(there, owner)
+    pass_steps(steps[:4], h)
     loads[1].wait()
     tiles(first_up)
-    for there, owner, _, _ in steps[4:]:
-        pass_step(there, owner)
-    for owner in range(chips):
-        from_core(1 - h, chips, owner)
+    pass_steps(steps[4:], h)
+    for b in range(2):
+        for owner in range(chips):
+            from_core(1 - h, chips, owner, b)
 
     def second(cols):
         g = gate_sum[:, cols] + product(1 - h, gate, cols)
@@ -421,6 +426,21 @@
         return (
             wy.at[rows_of(1 - c, b, dz)], core_in.at[dz, b], yc_s.at[dz, b], yc_r.at[dz, b], core
         )
+
+    def part_rows(other):
+        part = 1 - c if other else c
+        return pl.ds(pl.multiple_of(part * ROWS, ROWS), ROWS)
+
+    def side_link(dz, other):
+        rows, o = part_rows(other), int(other)
+        return (
+            side_out.at[dz, rows], side_in.at[dz, rows], yx_s.at[dz, o], yx_r.at[dz, o], side
+        )
+
+    def owner_rows(side_half, b, dz, other):
+        part = 1 - c if other else c
+        first = side_half * 2 * span + b * span + ROWS * (2 * at_z(dz) + part)
+        return pl.ds(pl.multiple_of(first, ROWS), ROWS)
 
     lower(1 - c)
     for b in (1 - h, h):
@@ -432,26 +452,26 @@
         side_out[dz] = (
             wy[rows_of(c, 1 - h, dz)].astype(F32) + core_in[dz, 1 - h].astype(F32)
         ).astype(BF)
-        send(side_out.at[dz], side_in.at[dz], yx_s.at[dz], yx_r.at[dz], side)
+        for other in (False, True):
+            send(*side_link(dz, other))
 
     def out_link(dz, other):
-        if dz:
-            part = 1 - c if other else c
-            src = ready.at[dz, pl.ds(pl.multiple_of(part * ROWS, ROWS), ROWS)]
-        else:
-            src = ready.at[dz, pl.ds(pl.multiple_of((1 - c) * ROWS, ROWS), ROWS)]
         o = int(other)
-        return (src, back.at[dz, o], yz_s.at[dz, o], yz_r.at[dz, o], to(dz, other))
+        return (
+            ready.at[dz, part_rows(other)], back.at[dz, o], yz_s.at[dz, o], yz_r.at[dz, o],
+            to(dz, other),
+        )
 
     for dz in order:
-        link(side_out.at[dz], side_in.at[dz], yx_s.at[dz], yx_r.at[dz], side).wait_recv()
         link(*core_link(dz, h)).wait_recv()
-        ready[dz] = (
-            wy[rows_of(c, h, dz)].astype(F32)
-            + core_in[dz, h].astype(F32)
-            + side_in[dz].astype(F32)
-        ).astype(BF)
         for other in (False, True):
+            rows = part_rows(other)
+            link(*side_link(dz, other)).wait_recv()
+            ready[dz, rows] = (
+                wy[owner_rows(c, h, dz, other)].astype(F32)
+                + core_in[dz, h, rows].astype(F32)
+                + side_in[dz, rows].astype(F32)
+            ).astype(BF)
             if dz or other:
                 send(*out_link(dz, other))
 
@@ -499,21 +519,22 @@
 
     for i in range(count):
         heads_link(i, h).wait_send()
-    for side_way, slot in ((1, 0), (-1, chips - 1)):
-        @pl.when(goes_on(side_way))
-        def _():
-            along(side_way, z, slot).wait_send()
-
-    for there, owner, slot, side_way in steps:
-        if slot % (chips - 1) < chips - 2:
-            @pl.when(there & goes_on(side_way))
+    for b in range(2):
+        for side_way, slot in ((1, 0), (-1, chips - 1)):
+            @pl.when(goes_on(side_way))
             def _():
-                along(side_way, owner, slot + 1).wait_send()
-
-    for owner in range(chips):
-        to_side(owner).wait_send()
-        to_core(h, 0, owner).wait_send()
-        to_core(1 - h, chips, owner).wait_send()
+                along(side_way, z, slot, b).wait_send()
+
+        for there, owner, slot, side_way in steps:
+            if slot % (chips - 1) < chips - 2:
+                @pl.when(there & goes_on(side_way))
+                def _():
+                    along(side_way, owner, slot + 1, b).wait_send()
+
+        for owner in range(chips):
+            to_side(owner, b).wait_send()
+            to_core(h, 0, owner, b).wait_send()
+            to_core(1 - h, chips, owner, b).wait_send()
 
 
 def per_device_fused(
@@ -559,8 +580,8 @@
             vmem((4, 2, ROWS, half), BF),
             sem((4,)), sem((count,)), sem((count,)), sem((count,)), sem((count,)), sem((1,)), sem((1,)),
             sem((4, 2)), sem((4, 2)), sem((3, 2)), sem((3, 2)),
-            sem((6,)), sem((6,)), sem((4,)), sem((4,)), sem((8,)), sem((8,)),
-            sem((4, 2)), sem((4, 2)), sem((4,)), sem((4,)), sem((4, 2)), sem((4, 2)),
+            sem((6, 2)), sem((6, 2)), sem((4, 2)), sem((4, 2)), sem((8, 2)), sem((8, 2)),
+            sem((4, 2)), sem((4, 2)), sem((4, 2)), sem((4, 2)), sem((4, 2)), sem((4, 2)),
         ],
         compiler_params=pltpu.CompilerParams(
             collective_id=0, has_side_effects=True, vmem_limit_bytes=VMEM_BYTES

time: 96.1 us -> 93.1 us (0.969)
  Pallas kernels: 93.4 us -> 91.2 us
    pallas_call x1, Pallas kernels: 93.4 us -> 91.2 us  [per_device_fused(): pl.pallas_call(layer_kernel, out_shape=jax.ShapeDtypeStruct(residual.shap...]
where the time goes in v3:
time: 93.1 us; the launch traced here: 92.8 us
  Pallas kernels  91.2 us (98%)
  local copies, waits for them, and re-layouts  1.62 us (2%)
    pallas_call x1, Pallas kernels, per_device_fused(): pl.pallas_call(layer_kernel, out_shape=jax.ShapeDtypeStruct(residual.shap...  91.2 us

profile of v3, /device:TPU:0, one launch (start us, length us, event | category | flops | bytes accessed | tf_op | source)
XLA Modules:
  0.0 92.8 jit_solution(12411274438548374873)
XLA Ops:
  0.0 91.2 %shard_map.100 = bf16[16,6144]{1,0:T(8,128)(2,1)} custom-call(bf16[128,512]{1,0:T(8,128)(2,1)} %q_ref.1, bf16[128,512]{1,0:T(8,128)(2,1)} %k_ref.1, bf16[128,512]{1,0:T(8,128)(2,1)} %v_ref.1, bf16[16,6144]{1,0:T(8,128)(2,1)} %res_ref.1, bf16[512,3072]{1,0:T(8,128)(2,1)} %wo_hbm.1, bf16[4,6144]{1,0:T(4,128)(2,1)} %bitcast.2, s32[2,16]{1,0:T(2,128)} %bitcast.3, ...), custom_call_target="tpu_custom_call" | custom-call | tf_op jit(solution)/shard_map/pallas_call | solution.py:553
  91.2 1.6 %copy.12 = bf16[16,6144]{1,0:T(8,128)(2,1)} copy(bf16[16,6144]{1,0:T(8,128)(2,1)} %shard_map.100) | data formatting | bytes 393216
